TPU v7x, 32 devices: a whole 2x2x4 slice. The times are simulated.
32 devices in a mesh: src: 4 (over y, x), tgt: 8 (over z, core).
Axes of the slice: x: 2, y: 2, z: 4, core: 2. Of those that a mesh axis runs over, the one named last changes fastest.
Arguments:
- pcs_source: bfloat16 [30, 8192], P(None, 'src'), may hold values from -6 to 10
- pcs_target: bfloat16 [30, 16384], P(None, 'tgt'), may hold values from -6 to 6
- growth: float32 [8192], P('src'), may hold values from 0.25 to 4
- scores: bfloat16 [8192, 128], P('src'), may hold values from -6 to 6
Outputs:
- source_potential: float32 [8192], P('src')
- target_potential: float32 [16384], P('tgt')
- transported: float32 [16384, 128], P('tgt')
All inputs are finite; a program needn't handle non-finite values.
Results may differ from a plain program's by a relative error of at most 0.0029.
Values sent between devices are 32-bit elements; how exact they have to be, the bound alone decides.
A program may use at most 64 MiB of HBM per device.

v0:
```python
import math

import jax
import jax.numpy as jnp
from jax import lax
from jax.sharding import PartitionSpec as P

ITERS = 2


EPSILON = 0.05
MARGIN = 1.0
FACTOR = MARGIN / (MARGIN + EPSILON)


def joined(value, axis, join):
    pieces = jax.tree.map(lambda part: lax.all_gather(part, axis), value)
    head = jax.tree.map(lambda part: part[0], pieces)
    tail = jax.tree.map(lambda part: part[1:], pieces)
    subtotal, _ = lax.scan(lambda subtotal, section: (join(subtotal, section), None), head, tail)
    return subtotal


def cost_tile(left, right, right_sq):
    cross = lax.dot_general(
        left, right, (((0,), (0,)), ((), ())), preferred_element_type=jnp.float32
    )
    left_wide = left.astype(jnp.float32)
    left_sq = jnp.sum(left_wide * left_wide, axis=0)
    return (left_sq[:, None] + right_sq[None, :] - 2.0 * cross) / left.shape[0]


def combine(first, second):
    peak = jnp.maximum(first[0], second[0])
    total = first[1] * jnp.exp(first[0] - peak) + second[1] * jnp.exp(second[0] - peak)
    return (peak, total)


def row_reduce(peak, total):
    top, summed = joined((peak, total), "tgt", combine)
    return top + jnp.log(summed)


def column_reduce(peak, total):
    top, summed = joined((peak, total), "src", combine)
    return top + jnp.log(summed)


def shards(pcs_source, pcs_target, growth, scores):
    source_rows = pcs_source.shape[1]
    target_rows = pcs_target.shape[1]
    width = math.gcd(source_rows, 512)
    count_blocks = source_rows // width
    source_blocks = jnp.transpose(
        pcs_source.reshape(pcs_source.shape[0], count_blocks, width), (1, 0, 2)
    )
    score_blocks = scores.reshape(count_blocks, width, scores.shape[1])
    total_sources = source_rows * lax.axis_size("src")
    total_targets = target_rows * lax.axis_size("tgt")
    log_a = jnp.log(growth) - jnp.log(jnp.float32(total_sources))
    log_b = -jnp.log(jnp.float32(total_targets))
    target_wide = pcs_target.astype(jnp.float32)
    target_sq = jnp.sum(target_wide * target_wide, axis=0)
    source_potential = jnp.zeros((source_rows,), jnp.float32)
    target_potential = jnp.zeros((target_rows,), jnp.float32)
    for step in range(ITERS):
        gpot = target_potential

        def row_stats(block):
            logits = (gpot[None, :] - cost_tile(block, pcs_target, target_sq)) / EPSILON
            peak = jnp.max(logits, axis=1)
            return (peak, jnp.sum(jnp.exp(logits - peak[:, None]), axis=1))

        peaks, totals = lax.map(row_stats, source_blocks)
        rows = row_reduce(peaks.reshape(-1), totals.reshape(-1))
        source_potential = FACTOR * (EPSILON * log_a - EPSILON * rows)

        def column_stats(carry, inputs):
            block, fblock = inputs
            logits = (fblock[:, None] - cost_tile(block, pcs_target, target_sq)) / EPSILON
            newpeak = jnp.maximum(carry[0], jnp.max(logits, axis=0))
            total = carry[1] * jnp.exp(carry[0] - newpeak) + jnp.sum(
                jnp.exp(logits - newpeak[None, :]), axis=0
            )
            return ((newpeak, total), None)

        start = (
            jnp.full((target_rows,), -jnp.inf, jnp.float32),
            jnp.zeros((target_rows,), jnp.float32),
        )
        (cpeak, ctotal), unused = lax.scan(
            column_stats, start, (source_blocks, source_potential.reshape(count_blocks, width))
        )
        columns = column_reduce(cpeak, ctotal)
        target_potential = FACTOR * (EPSILON * log_b - EPSILON * columns)

    def carry_scores(carry, inputs):
        block, fblock, sblock = inputs
        tile = cost_tile(block, pcs_target, target_sq)
        plan = jnp.exp((fblock[:, None] + target_potential[None, :] - tile) / EPSILON)
        mass = carry[1] + jnp.sum(plan, axis=0)
        carried = carry[0] + lax.dot_general(
            plan.astype(jnp.bfloat16),
            sblock,
            (((0,), (0,)), ((), ())),
            preferred_element_type=jnp.float32,
        )
        return ((carried, mass), None)

    start = (
        jnp.zeros((target_rows, scores.shape[1]), jnp.float32),
        jnp.zeros((target_rows,), jnp.float32),
    )
    (carried, mass), unused = lax.scan(
        carry_scores,
        start,
        (source_blocks, source_potential.reshape(count_blocks, width), score_blocks),
    )
    carried, mass = lax.psum((carried, mass), "src")
    transported = carried / mass[:, None]
    return (source_potential, target_potential, transported)


def solution(mesh):
    in_specs = (P(None, "src"), P(None, "tgt"), P("src"), P("src", None))
    out_specs = (P("src"), P("tgt"), P("tgt", None))
    return jax.shard_map(shards, mesh=mesh, in_specs=in_specs, out_specs=out_specs, check_vma=False)
```

profile of v0, /device:TPU:0, one launch (start us, length us, event | category | flops | bytes accessed | tf_op | source)
XLA Modules:
  0.0 262.5 jit_solution(15831868486675719388)
XLA Ops:
  9.2 12.1 %while.111 = (s32[]{:T(128)}, f32[4,512]{1,0:T(4,128)S(1)}, f32[4,512]{1,0:T(4,128)S(1)}, bf16[4,30,512]{2,1,0:T(8,128)(2,1)S(1)}, f32[2048]{0:T(1024)S(1)}, /*index=5*/bf16[30,2048]{1,0:T(8,128)(2,1)}, s32[]{:T(128)}, s32[]{:T(128)}) while((s32[]{:T(128)}, f32[4,512]{1,0:T(4,128)S(1)}, f32[4,512]{1,0:T(4,128)S(1)}, ...), condition=%wide.region_5.6_spmd, body=%wide.region_1.5_spmd.sunk | while | flops 72396288 | bytes 8601701 | solution.py:74
  21.4 15.7 %all-gather.4 = f32[8,1,2048]{2,1,0:T(1,128)S(1)} all-gather(f32[1,1,2048]{2,1,0:T(1,128)S(1)} %reshape.62), channel_id=1, replica_groups=mesh['src'=4,'tgt'=8] {'tgt'}, dimensions={0}, use_global_device_ids=true | all-gather | bytes 73728 | tf_op jit(solution)/shard_map/all_gather | solution.py:17
  37.1 14.0 %all-gather.5 = f32[8,1,2048]{2,1,0:T(1,128)S(1)} all-gather(f32[1,1,2048]{2,1,0:T(1,128)S(1)} %reshape.64), channel_id=1, replica_groups=mesh['src'=4,'tgt'=8] {'tgt'}, dimensions={0}, use_global_device_ids=true | all-gather | bytes 73728 | tf_op jit(solution)/shard_map/all_gather | solution.py:17
  51.6 27.6 %while.117 = (s32[]{:T(128)}, f32[2048]{0:T(1024)S(1)}, f32[2048]{0:T(1024)S(1)}, f32[4,512]{1,0:T(4,128)S(1)}, bf16[4,30,512]{2,1,0:T(8,128)(2,1)S(1)}, /*index...) while((s32[]{:T(128)}, f32[2048]{0:T(1024)S(1)}, f32[2048]{0:T(1024)S(1)}, ...), condition=%wide.region_12.13_spmd.clone, body=%wide.region_8.12_spmd.clone.sunk | while | flops 72407552 | bytes 8700020 | solution.py:91
  51.7 4.0 %fusion.51 = (f32[2048]{0:T(1024)S(1)}, f32[512,2048]{1,0:T(8,128)}) fusion(bf16[30,2048]{1,0:T(8,128)(2,1)} %get-tuple-element.1081, bf16[4,30,512]{2,1,0:T(8,128)(2,1)S(1)} %get-tuple-element.1079, s32[]{:T(128)} %get-tuple-element.1066, f32[2048]{0:T(1024)S(1)} %get-tuple-element.1080, f32[512]{0:T(512)S(1)} %multiply_reduce_fusion.13, ...), kind=kOutput, calls=%fused_computation.69.clone.1 | convolution fusion | flops 70252544 | bytes 4370436 | tf_op jit(solution)/shard_map/while/body/eval_jaxpr/dot_general | solution.py:25
  58.6 4.0 %fusion.51 = (f32[2048]{0:T(1024)S(1)}, f32[512,2048]{1,0:T(8,128)}) fusion(bf16[30,2048]{1,0:T(8,128)(2,1)} %get-tuple-element.1081, bf16[4,30,512]{2,1,0:T(8,128)(2,1)S(1)} %get-tuple-element.1079, s32[]{:T(128)} %get-tuple-element.1066, f32[2048]{0:T(1024)S(1)} %get-tuple-element.1080, f32[512]{0:T(512)S(1)} %multiply_reduce_fusion.13, ...), kind=kOutput, calls=%fused_computation.69.clone.1 | convolution fusion | flops 70252544 | bytes 4370436 | tf_op jit(solution)/shard_map/while/body/eval_jaxpr/dot_general | solution.py:25
  62.6 2.8 %exponential_reduce_fusion.10 = f32[2048]{0:T(1024)S(1)} fusion(f32[512,2048]{1,0:T(8,128)} %get-tuple-element.994, f32[2048]{0:T(1024)S(1)} %select_maximum_fusion.4), kind=kLoop, calls=%fused_computation.24.clone.1 | loop fusion | flops 2095104 | bytes 4210688 | tf_op jit(solution)/shard_map/while/body/eval_jaxpr/reduce_sum | solution.py:82
  65.5 4.0 %fusion.51 = (f32[2048]{0:T(1024)S(1)}, f32[512,2048]{1,0:T(8,128)}) fusion(bf16[30,2048]{1,0:T(8,128)(2,1)} %get-tuple-element.1081, bf16[4,30,512]{2,1,0:T(8,128)(2,1)S(1)} %get-tuple-element.1079, s32[]{:T(128)} %get-tuple-element.1066, f32[2048]{0:T(1024)S(1)} %get-tuple-element.1080, f32[512]{0:T(512)S(1)} %multiply_reduce_fusion.13, ...), kind=kOutput, calls=%fused_computation.69.clone.1 | convolution fusion | flops 70252544 | bytes 4370436 | tf_op jit(solution)/shard_map/while/body/eval_jaxpr/dot_general | solution.py:25
  72.4 4.0 %fusion.51 = (f32[2048]{0:T(1024)S(1)}, f32[512,2048]{1,0:T(8,128)}) fusion(bf16[30,2048]{1,0:T(8,128)(2,1)} %get-tuple-element.1081, bf16[4,30,512]{2,1,0:T(8,128)(2,1)S(1)} %get-tuple-element.1079, s32[]{:T(128)} %get-tuple-element.1066, f32[2048]{0:T(1024)S(1)} %get-tuple-element.1080, f32[512]{0:T(512)S(1)} %multiply_reduce_fusion.13, ...), kind=kOutput, calls=%fused_computation.69.clone.1 | convolution fusion | flops 70252544 | bytes 4370436 | tf_op jit(solution)/shard_map/while/body/eval_jaxpr/dot_general | solution.py:25
  79.2 8.2 %all-gather = f32[8192]{0:T(1024)S(1)} all-gather(f32[2048]{0:T(1024)S(1)} %get-tuple-element.314), channel_id=2, replica_groups=mesh['src'=4,'tgt'=8] {'src'}, dimensions={0}, use_global_device_ids=true | all-gather | bytes 40960 | tf_op jit(solution)/shard_map/all_gather | solution.py:17
  87.5 8.2 %all-gather.1 = f32[8192]{0:T(1024)S(1)} all-gather(f32[2048]{0:T(1024)S(1)} %get-tuple-element.315), channel_id=3, replica_groups=mesh['src'=4,'tgt'=8] {'src'}, dimensions={0}, use_global_device_ids=true | all-gather | bytes 40960 | tf_op jit(solution)/shard_map/all_gather | solution.py:17
  95.9 12.2 %while.114 = (s32[]{:T(128)}, f32[4,512]{1,0:T(4,128)S(1)}, f32[4,512]{1,0:T(4,128)S(1)}, f32[2048]{0:T(1024)S(1)}, bf16[4,30,512]{2,1,0:T(8,128)(2,1)S(1)}, /*i...) while((s32[]{:T(128)}, f32[4,512]{1,0:T(4,128)S(1)}, f32[4,512]{1,0:T(4,128)S(1)}, ...), condition=%wide.region_19.20_spmd, body=%wide.region_15.19_spmd.sunk | while | flops 72396288 | bytes 8609901 | solution.py:74
  108.1 14.0 %all-gather.6 = f32[8,1,2048]{2,1,0:T(1,128)S(1)} all-gather(f32[1,1,2048]{2,1,0:T(1,128)S(1)} %reshape.66), channel_id=1, replica_groups=mesh['src'=4,'tgt'=8] {'tgt'}, dimensions={0}, use_global_device_ids=true | all-gather | bytes 73728 | tf_op jit(solution)/shard_map/all_gather | solution.py:17
  122.2 14.0 %all-gather.7 = f32[8,1,2048]{2,1,0:T(1,128)S(1)} all-gather(f32[1,1,2048]{2,1,0:T(1,128)S(1)} %reshape.68), channel_id=1, replica_groups=mesh['src'=4,'tgt'=8] {'tgt'}, dimensions={0}, use_global_device_ids=true | all-gather | bytes 73728 | tf_op jit(solution)/shard_map/all_gather | solution.py:17
  137.3 27.6 %while.118 = (s32[]{:T(128)}, f32[2048]{0:T(1024)S(1)}, f32[2048]{0:T(1024)S(1)}, f32[4,512]{1,0:T(4,128)S(1)}, bf16[4,30,512]{2,1,0:T(8,128)(2,1)S(1)}, /*index...) while((s32[]{:T(128)}, f32[2048]{0:T(1024)S(1)}, f32[2048]{0:T(1024)S(1)}, ...), condition=%wide.region_26.27_spmd.clone, body=%wide.region_22.26_spmd.clone.sunk | while | flops 72407552 | bytes 8700020 | solution.py:91
  137.3 4.0 %fusion.54 = (f32[2048]{0:T(1024)S(1)}, f32[512,2048]{1,0:T(8,128)}) fusion(bf16[30,2048]{1,0:T(8,128)(2,1)} %get-tuple-element.1171, bf16[4,30,512]{2,1,0:T(8,128)(2,1)S(1)} %get-tuple-element.1169, s32[]{:T(128)} %get-tuple-element.1156, f32[2048]{0:T(1024)S(1)} %get-tuple-element.1170, f32[512]{0:T(512)S(1)} %multiply_reduce_fusion.14, ...), kind=kOutput, calls=%fused_computation.70.clone.1 | convolution fusion | flops 70252544 | bytes 4370436 | tf_op jit(solution)/shard_map/while/body/eval_jaxpr/dot_general | solution.py:25
  144.2 4.0 %fusion.54 = (f32[2048]{0:T(1024)S(1)}, f32[512,2048]{1,0:T(8,128)}) fusion(bf16[30,2048]{1,0:T(8,128)(2,1)} %get-tuple-element.1171, bf16[4,30,512]{2,1,0:T(8,128)(2,1)S(1)} %get-tuple-element.1169, s32[]{:T(128)} %get-tuple-element.1156, f32[2048]{0:T(1024)S(1)} %get-tuple-element.1170, f32[512]{0:T(512)S(1)} %multiply_reduce_fusion.14, ...), kind=kOutput, calls=%fused_computation.70.clone.1 | convolution fusion | flops 70252544 | bytes 4370436 | tf_op jit(solution)/shard_map/while/body/eval_jaxpr/dot_general | solution.py:25
  151.1 4.0 %fusion.54 = (f32[2048]{0:T(1024)S(1)}, f32[512,2048]{1,0:T(8,128)}) fusion(bf16[30,2048]{1,0:T(8,128)(2,1)} %get-tuple-element.1171, bf16[4,30,512]{2,1,0:T(8,128)(2,1)S(1)} %get-tuple-element.1169, s32[]{:T(128)} %get-tuple-element.1156, f32[2048]{0:T(1024)S(1)} %get-tuple-element.1170, f32[512]{0:T(512)S(1)} %multiply_reduce_fusion.14, ...), kind=kOutput, calls=%fused_computation.70.clone.1 | convolution fusion | flops 70252544 | bytes 4370436 | tf_op jit(solution)/shard_map/while/body/eval_jaxpr/dot_general | solution.py:25
  158.0 4.0 %fusion.54 = (f32[2048]{0:T(1024)S(1)}, f32[512,2048]{1,0:T(8,128)}) fusion(bf16[30,2048]{1,0:T(8,128)(2,1)} %get-tuple-element.1171, bf16[4,30,512]{2,1,0:T(8,128)(2,1)S(1)} %get-tuple-element.1169, s32[]{:T(128)} %get-tuple-element.1156, f32[2048]{0:T(1024)S(1)} %get-tuple-element.1170, f32[512]{0:T(512)S(1)} %multiply_reduce_fusion.14, ...), kind=kOutput, calls=%fused_computation.70.clone.1 | convolution fusion | flops 70252544 | bytes 4370436 | tf_op jit(solution)/shard_map/while/body/eval_jaxpr/dot_general | solution.py:25
  164.9 7.2 %all-gather.2 = f32[8192]{0:T(1024)S(1)} all-gather(f32[2048]{0:T(1024)S(1)} %get-tuple-element.322), channel_id=4, replica_groups=mesh['src'=4,'tgt'=8] {'src'}, dimensions={0}, use_global_device_ids=true | all-gather | bytes 40960 | tf_op jit(solution)/shard_map/all_gather | solution.py:17
  172.1 8.3 %all-gather.3 = f32[8192]{0:T(1024)S(1)} all-gather(f32[2048]{0:T(1024)S(1)} %get-tuple-element.323), channel_id=5, replica_groups=mesh['src'=4,'tgt'=8] {'src'}, dimensions={0}, use_global_device_ids=true | all-gather | bytes 40960 | tf_op jit(solution)/shard_map/all_gather | solution.py:17
  180.7 18.7 %while.119 = (s32[]{:T(128)}, f32[2048,128]{1,0:T(8,128)S(1)}, f32[2048]{0:T(1024)S(1)}, f32[4,512]{1,0:T(4,128)S(1)}, f32[2048]{0:T(1024)S(1)}, /*index=5*/bf16...) while((s32[]{:T(128)}, f32[2048,128]{1,0:T(8,128)S(1)}, ...), condition=%wide.region_32.33_spmd.clone, body=%wide.region_29.32_spmd.clone.sunk | while | flops 341359104 | bytes 6668932 | solution.py:114
  200.4 9.2 %psum.15 = f32[2048]{0:T(1024)S(1)} all-reduce(f32[2048]{0:T(1024)S(1)} %get-tuple-element.327), channel_id=1, replica_groups=mesh['src'=4,'tgt'=8] {'src'}, use_global_device_ids=true, to_apply=%region_34.35 | all-reduce | flops 2048 | bytes 16384 | tf_op jit(solution)/shard_map/psum | solution.py:119
  209.6 43.5 %all-reduce.2.cloned.1.call-done = f32[2048,128]{1,0:T(8,128)} async-done(((f32[2048,128]{1,0:T(8,128)}), f32[2048,128]{1,0:T(8,128)}) %all-reduce.2.cloned.1.call-update) | async-done | bytes 1048592 | tf_op jit(solution)/shard_map/psum | solution.py:119
  (209 shorter events, 70.9 us)
Async XLA Ops:
  7.2 245.9 %all-reduce.2.cloned.1.call-start = ((), (), s32[]{:S(2)}) async-start(), calls=%async_computation | async-start | bytes 2097152 | tf_op jit(solution)/shard_map/psum | solution.py:119
  9.2 42.4 %copy-start.2 = (f32[2048]{0:T(1024)S(1)}, f32[2048]{0:T(1024)}, u32[]{:S(2)}) copy-start(f32[2048]{0:T(1024)} %param.24) | copy-start | bytes 24580
  136.7 0.6 copy-start.1
  199.4 1.0 copy-start
  199.4 56.2 %copy-start.3 = (f32[2048]{0:T(1024)}, f32[2048]{0:T(1024)S(1)}, u32[]{:S(2)}) copy-start(f32[2048]{0:T(1024)S(1)} %get-tuple-element.1242) | copy-start | bytes 24580
Sparse Core Ops, SparseCore 0:
  200.5 52.5 all-reduce.1
where the time goes:
time: 264 us; the launch traced here: 262 us
  blocking collectives  98.8 us (37%)
  matrix products  67.9 us (26%)
  waiting for transfers between devices  43.5 us (16%)
  other arithmetic  32.5 us (12%)
  between operations  14.4 us (5%)
  local copies, waits for them, and re-layouts  4.16 us (2%)
    all_gather x8, blocking collectives, joined(): pieces = jax.tree.map(lambda part: lax.all_gather(part, axis), value)  89.6 us
    dot_general x20, matrix products, cost_tile(): lax.dot_general(left, right, (((0,), (0,)), ((), ())), preferred_element_...  60.1 us
    psum x1, waiting for transfers between devices, shards(): carried, mass = lax.psum((carried, mass), 'src')  43.5 us
    reduce_sum x8, other arithmetic, column_stats(): jnp.sum(jnp.exp(logits - newpeak[None, :]), axis=0)  22.2 us
    psum x1, blocking collectives, shards(): carried, mass = lax.psum((carried, mass), 'src')  9.18 us
    dot_general x4, matrix products, carry_scores(): lax.dot_general(plan.astype(jnp.bfloat16), sblock, (((0,), (0,)), ((), ()...  7.8 us
    reduce_sum x8, other arithmetic, row_stats(): return (peak, jnp.sum(jnp.exp(logits - peak[:, None]), axis=1))  5.69 us
  transfers between devices with their start and end apart: 1, of which 1 were waited for; matrix products, arithmetic and copies ran while one was open for 0% of the time, Pallas kernels for 0%

commit v1 on v0

v1 whole, which is shorter than its diff:
```python
import functools
import math

import jax
import jax.numpy as jnp
from jax import lax
from jax.experimental import pallas as pl
from jax.experimental.pallas import tpu as pltpu
from jax.sharding import PartitionSpec as P

ITERS = 2
EPSILON = 0.05
MARGIN = 1.0
FACTOR = MARGIN / (MARGIN + EPSILON)
LANES = 128
LOG2E = math.log2(math.e)
UNIT = EPSILON / LOG2E
MESH = pl.DeviceIdType.MESH


def augment(coords_ref, wide_ref, rows_ref, columns_ref, norm_first):
    pcs, cells = coords_ref.shape
    wide = coords_ref[...].astype(jnp.float32)
    norm = -0.5 * jnp.sum(wide * wide, axis=0, keepdims=True)
    high = norm.astype(jnp.bfloat16).astype(jnp.float32)
    mid = (norm - high).astype(jnp.bfloat16).astype(jnp.float32)
    low = norm - high - mid
    base = -(-pcs // 8) * 8
    at = lax.broadcasted_iota(jnp.int32, (8, cells), 0) - (0 if norm_first else 3)
    one = jnp.where((at >= 3) & (at < 6) if norm_first else (at < 0), 1.0, 0.0)
    extra = jnp.where(at == 0, high, jnp.where(at == 1, mid, jnp.where(at == 2, low, one)))
    wide_ref[...] = jnp.zeros(wide_ref.shape, jnp.float32)
    wide_ref[0:pcs, :] = wide
    wide_ref[base : base + 8, :] = extra
    for k in range(cells // LANES):
        cut = slice(k * LANES, (k + 1) * LANES)
        piece = wide_ref[:, cut]
        rows_ref[cut, :] = piece.T.astype(jnp.bfloat16)
        columns_ref[:, cut] = piece.astype(jnp.bfloat16)


def spread(dense, out_ref):
    for k in range(dense.shape[0]):
        out_ref[k * LANES : (k + 1) * LANES, :] = jnp.broadcast_to(
            dense[k : k + 1, :], (LANES, LANES)
        ).T


def join(peak, total, block):
    t = block.reshape(-1, 8, LANES)
    newpeak = jnp.maximum(peak, jnp.max(t, axis=0))
    total = total * jnp.exp2(peak - newpeak) + jnp.sum(jnp.exp2(t - newpeak[None]), axis=0)
    return newpeak, total


def closed(peak, total):
    top = jnp.max(peak, axis=0, keepdims=True)
    return top, jnp.sum(total * jnp.exp2(peak - top), axis=0, keepdims=True)


def column_pass(tile_ref, bias_ref, lse_ref, make=None):
    rows, columns = tile_ref.shape
    width = math.gcd(columns, 256)
    step = math.gcd(rows, 256)
    sub = math.gcd(step, 128)
    halves = width // LANES

    def over_columns(c, unused):
        start = pl.multiple_of(c * width, width)

        def over_rows(r, carry):
            row = pl.multiple_of(r * step, step)
            if make is not None:
                tile_ref[pl.ds(row, step), pl.ds(start, width)] = make(
                    pl.ds(row, step), pl.ds(start, width)
                )
            carry = list(carry)
            for q in range(step // sub):
                at = pl.ds(pl.multiple_of(row + q * sub, sub), sub)
                for h in range(halves):
                    lanes = pl.ds(pl.multiple_of(start + h * LANES, LANES), LANES)
                    block = tile_ref[at, lanes]
                    if bias_ref is not None:
                        block = block + bias_ref[at, :]
                    carry[h] = join(*carry[h], block)
            return tuple(carry)

        empty = (jnp.full((8, LANES), -jnp.inf, jnp.float32), jnp.zeros((8, LANES), jnp.float32))
        stats = lax.fori_loop(0, rows // step, over_rows, (empty,) * halves)
        for h in range(halves):
            top, total = closed(*stats[h])
            lse_ref[pl.ds(c * halves + h, 1), :] = top + jnp.log2(total)
        return unused

    lax.fori_loop(0, columns // width, over_columns, 0)


def kernel(
    n_src, n_tgt, xs_ref, yt_ref, growth_ref, scores_ref, f_ref, g_ref, out_ref,
    tile, tile_t, wide, x_rows, x_cols, y_rows, y_cols, scores_t, bias, weights, carried, partial,
    lse, row_buf, col_buf, stat, received, row_send, row_recv, col_send, col_recv,
    stat_send, stat_recv, part_send, part_recv, out_send, out_recv,
):
    src, tgt = lax.axis_index("src"), lax.axis_index("tgt")
    barrier = pltpu.get_barrier_semaphore()
    for k in range(1, n_src):
        pl.semaphore_signal(
            barrier, inc=1, device_id={"src": lax.rem(src + k, n_src)}, device_id_type=MESH
        )
    for k in range(1, n_tgt):
        pl.semaphore_signal(
            barrier, inc=1, device_id={"tgt": lax.rem(tgt + k, n_tgt)}, device_id_type=MESH
        )

    rows, columns = tile.shape
    scale = 2.0 * LOG2E / (xs_ref.shape[0] * EPSILON)
    augment(xs_ref, wide.at[:, 0:rows], x_rows, x_cols, False)
    augment(yt_ref, wide.at[:, 0:columns], y_rows, y_cols, True)

    def filled(left, right):
        def make(at, lanes):
            return scale * lax.dot_general(
                left[at, :], right[:, lanes], (((1,), (0,)), ((), ())),
                preferred_element_type=jnp.float32,
            )
        return make

    def exchange(buf, axis, me, n, send, recv):
        copies = [
            pltpu.make_async_remote_copy(
                src_ref=buf.at[me], dst_ref=buf.at[me], send_sem=send.at[k], recv_sem=recv.at[k],
                device_id={axis: lax.rem(me + k, n)}, device_id_type=MESH,
            )
            for k in range(1, n)
        ]
        for copy in copies:
            copy.start()
        return copies

    def joined(buf, n):
        parts = [buf[d] for d in range(n)]
        top = functools.reduce(jnp.maximum, parts)
        return top + jnp.log2(sum(jnp.exp2(part - top) for part in parts))

    log_a = jnp.log2(growth_ref[...]) - math.log2(rows * n_src)
    log_b = -math.log2(columns * n_tgt)
    for step in range(ITERS):
        first = step == 0
        column_pass(
            tile_t, None if first else bias.at[0:columns, :], row_buf.at[step, tgt],
            filled(y_rows, x_cols) if first else None,
        )
        if first:
            pl.semaphore_wait(barrier, n_src + n_tgt - 2)
        copies = exchange(row_buf.at[step], "tgt", tgt, n_tgt, row_send.at[step], row_recv.at[step])
        if first:
            for k in range(rows // LANES):
                cut = slice(k * LANES, (k + 1) * LANES)
                scores_t[:, cut] = scores_ref[cut, :].astype(jnp.float32).T.astype(jnp.bfloat16)
        for copy in copies:
            copy.wait()
        potential = FACTOR * (log_a - joined(row_buf.at[step], n_tgt))
        spread(potential, bias)
        if step < ITERS - 1:
            column_pass(
                tile, bias.at[0:rows, :], col_buf.at[step, src],
                filled(x_rows, y_cols) if first else None,
            )
            copies = exchange(
                col_buf.at[step], "src", src, n_src, col_send.at[step], col_recv.at[step]
            )
            for copy in copies:
                copy.wait()
            spread(FACTOR * (log_b - joined(col_buf.at[step], n_src)), bias)
    f_ref[...] = UNIT * potential

    piece = columns // n_src
    width = math.gcd(piece, 256)
    depth = math.gcd(rows, 256)
    halves = width // LANES
    sub = math.gcd(depth, 128)
    parts = []
    for k in range(1, n_src + 1):
        owner = lax.rem(src + k, n_src)

        def over_tiles(c, unused, owner=owner):
            start = pl.multiple_of(owner * piece + c * width, width)

            def tops(r, peaks):
                at = pl.ds(pl.multiple_of(r * depth, depth), depth)
                peaks = list(peaks)
                for h in range(halves):
                    lanes = pl.ds(pl.multiple_of(start + h * LANES, LANES), LANES)
                    block = tile[at, lanes] + bias[at, :]
                    peaks[h] = jnp.maximum(peaks[h], jnp.max(block.reshape(-1, 8, LANES), axis=0))
                return tuple(peaks)

            peaks = lax.fori_loop(
                0, rows // depth, tops,
                (jnp.full((8, LANES), -jnp.inf, jnp.float32),) * halves,
            )
            peaks = [jnp.max(peak, axis=0, keepdims=True) for peak in peaks]

            def plan(r, totals):
                row = pl.multiple_of(r * depth, depth)
                totals = list(totals)
                for q in range(depth // sub):
                    at = pl.ds(pl.multiple_of(row + q * sub, sub), sub)
                    for h in range(halves):
                        lanes = pl.ds(pl.multiple_of(start + h * LANES, LANES), LANES)
                        w = jnp.exp2(tile[at, lanes] + bias[at, :] - peaks[h])
                        totals[h] = totals[h] + jnp.sum(w.reshape(-1, 8, LANES), axis=0)
                        weights[at, h * LANES : (h + 1) * LANES] = w.astype(jnp.bfloat16)
                return tuple(totals)

            totals = lax.fori_loop(
                0, rows // depth, plan, (jnp.zeros((8, LANES), jnp.float32),) * halves
            )
            carried[...] = jnp.dot(scores_t[...], weights[...], preferred_element_type=jnp.float32)
            for h in range(halves):
                stat[src, 0, pl.ds(start // LANES + h, 1), :] = jnp.sum(
                    totals[h], axis=0, keepdims=True
                )
                stat[src, 1, pl.ds(start // LANES + h, 1), :] = peaks[h]
                at = pl.ds(pl.multiple_of(start + h * LANES, LANES), LANES)
                partial[at, :] = carried[:, h * LANES : (h + 1) * LANES].T
            return unused

        lax.fori_loop(0, piece // width, over_tiles, 0)
        if k < n_src:
            copy = pltpu.make_async_remote_copy(
                src_ref=partial.at[pl.ds(pl.multiple_of(owner * piece, piece), piece), :],
                dst_ref=received.at[k], send_sem=part_send.at[k], recv_sem=part_recv.at[k],
                device_id={"src": owner}, device_id_type=MESH,
            )
            copy.start()
            parts.append(copy)
    copies = exchange(stat, "src", src, n_src, stat_send, stat_recv)
    for copy in copies:
        copy.wait()
    peak = functools.reduce(jnp.maximum, [stat[d, 1] for d in range(n_src)])
    total = sum(stat[d, 0] * jnp.exp2(stat[d, 1] - peak) for d in range(n_src))
    g_ref[...] = UNIT * FACTOR * (log_b - (peak + jnp.log2(total)))
    for d in range(n_src):
        stat[d, 0] = jnp.exp2(stat[d, 1] - peak) / total
    for copy in parts:
        copy.wait()
    first_row = src * (piece // LANES)
    for q in range(piece // LANES):
        mine = pl.ds(pl.multiple_of(src * piece + q * LANES, LANES), LANES)
        result = None
        for k in range(n_src):
            sender = lax.rem(src - k + n_src, n_src)
            share = jnp.broadcast_to(
                stat[sender, 0, pl.ds(first_row + q, 1), :], (LANES, LANES)
            ).T
            block = partial[mine, :] if k == 0 else received[k, q * LANES : (q + 1) * LANES, :]
            result = share * block if result is None else result + share * block
        out_ref[mine, :] = result
    mine = pl.ds(pl.multiple_of(src * piece, piece), piece)
    copies = [
        pltpu.make_async_remote_copy(
            src_ref=out_ref.at[mine, :], dst_ref=out_ref.at[mine, :],
            send_sem=out_send.at[k], recv_sem=out_recv.at[k],
            device_id={"src": lax.rem(src + k, n_src)}, device_id_type=MESH,
        )
        for k in range(1, n_src)
    ]
    for copy in copies:
        copy.start()
    for copy in copies:
        copy.wait()


def solution(mesh):
    n_src, n_tgt = mesh.shape["src"], mesh.shape["tgt"]

    def shards(pcs_source, pcs_target, growth, scores):
        rows, columns = pcs_source.shape[1], pcs_target.shape[1]
        programs = scores.shape[1]
        piece = columns // n_src
        f32, bf16 = jnp.float32, jnp.bfloat16
        sem = pltpu.SemaphoreType.DMA
        whole = pl.BlockSpec(memory_space=pltpu.VMEM)
        dense_r, dense_c = (rows // LANES, LANES), (columns // LANES, LANES)
        f, g, out = pl.pallas_call(
            functools.partial(kernel, n_src, n_tgt),
            out_shape=(
                jax.ShapeDtypeStruct(dense_r, f32),
                jax.ShapeDtypeStruct(dense_c, f32),
                jax.ShapeDtypeStruct((columns, programs), f32),
            ),
            in_specs=[whole] * 4,
            out_specs=(whole,) * 3,
            scratch_shapes=[
                pltpu.VMEM((rows, columns), f32),
                pltpu.VMEM((columns, rows), f32),
                pltpu.VMEM((LANES, max(rows, columns)), f32),
                pltpu.VMEM((rows, LANES), bf16),
                pltpu.VMEM((LANES, rows), bf16),
                pltpu.VMEM((columns, LANES), bf16),
                pltpu.VMEM((LANES, columns), bf16),
                pltpu.VMEM((programs, rows), bf16),
                pltpu.VMEM((max(rows, columns), LANES), f32),
                pltpu.VMEM((rows, math.gcd(piece, 256)), bf16),
                pltpu.VMEM((programs, math.gcd(piece, 256)), f32),
                pltpu.VMEM((columns, programs), f32),
                pltpu.VMEM((8, LANES), f32),
                pltpu.VMEM((ITERS, n_tgt) + dense_r, f32),
                pltpu.VMEM((ITERS, n_src) + dense_c, f32),
                pltpu.VMEM((n_src, 2) + dense_c, f32),
                pltpu.VMEM((n_src, piece, programs), f32),
                sem((ITERS, n_tgt)),
                sem((ITERS, n_tgt)),
                sem((ITERS, n_src)),
                sem((ITERS, n_src)),
                sem((n_src,)),
                sem((n_src,)),
                sem((n_src,)),
                sem((n_src,)),
                sem((n_src,)),
                sem((n_src,)),
            ],
            compiler_params=pltpu.CompilerParams(
                collective_id=0, has_side_effects=True, vmem_limit_bytes=60 * 2**20
            ),
            name="coupling",
        )(pcs_source, pcs_target, growth.reshape(dense_r), scores)
        return f.reshape(-1), g.reshape(-1), out

    in_specs = (P(None, "src"), P(None, "tgt"), P("src"), P("src", None))
    out_specs = (P("src"), P("tgt"), P("tgt", None))
    return jax.shard_map(shards, mesh=mesh, in_specs=in_specs, out_specs=out_specs, check_vma=False)
```

time: 264 us -> 90.7 us (0.34)
  blocking collectives: 98.8 us -> 0 us
  Pallas kernels: 0 us -> 85.6 us
  matrix products: 67.9 us -> 0 us
  waiting for transfers between devices: 43.5 us -> 0 us
  other arithmetic: 32.5 us -> 0 us
  between operations: 14.4 us -> 0.65 us
    all_gather x8 -> x0, blocking collectives: 89.6 us -> none  [joined(): pieces = jax.tree.map(lambda part: lax.all_gather(part, axis), value)]
    pallas_call x0 -> x1, Pallas kernels: none -> 85.6 us  [shards(): pl.pallas_call(functools.partial(kernel, n_src, n_tgt), out_shape=(jax.Sh...]
    dot_general x24 -> x0, matrix products: 67.9 us -> none  [the longest x20 60.1 us: cost_tile(): lax.dot_general(left, right, (((0,), (0,)), ((), ())), preferred_element_...]
    psum x1 -> x0, waiting for transfers between devices: 43.5 us -> none  [shards(): carried, mass = lax.psum((carried, mass), 'src')]
    reduce_sum x37 -> x0, other arithmetic: 29.5 us -> none  [the longest x8 22.2 us: column_stats(): jnp.sum(jnp.exp(logits - newpeak[None, :]), axis=0)]
    psum x1 -> x0, blocking collectives: 9.18 us -> none  [shards(): carried, mass = lax.psum((carried, mass), 'src')]
  transfers between devices with their start and end apart: 1 -> 0, of which waited for: 1 -> 0; matrix products, arithmetic and copies ran while one was open for 0% -> 0% of each run, Pallas kernels for 0% -> 0%
where the time goes in v1:
time: 90.7 us; the launch traced here: 90.5 us
  Pallas kernels  85.6 us (94%)
  local copies, waits for them, and re-layouts  4.25 us (5%)
    pallas_call x1, Pallas kernels, shards(): pl.pallas_call(functools.partial(kernel, n_src, n_tgt), out_shape=(jax.Sh...  85.6 us
    unnamed x7, local copies, waits for them, and re-layouts  4.25 us

profile of v1, /device:TPU:0, one launch (start us, length us, event | category | flops | bytes accessed | tf_op | source)
XLA Modules:
  0.0 90.5 jit_solution(1151779949686229781)
XLA Ops:
  0.6 85.6 %coupling.1 = (f32[16,128]{1,0:T(8,128)}, f32[16,128]{1,0:T(8,128)}, f32[2048,128]{1,0:T(8,128)}) custom-call(bf16[30,2048]{1,0:T(8,128)(2,1)} %xs_ref.1, bf16[30,2048]{1,0:T(8,128)(2,1)} %yt_ref.1, f32[16,128]{1,0:T(8,128)} %bitcast.3, bf16[2048,128]{1,0:T(8,128)(2,1)} %scores_ref.1), custom_call_target="tpu_custom_call" | custom-call | tf_op jit(solution)/shard_map/coupling/pallas_call | solution.py:286
  86.2 0.0 copy-start.1
  86.2 0.7 copy-done.1
  86.9 0.0 copy-start
  86.9 0.6 copy.10
  87.5 0.1 copy-done
  87.6 0.6 copy.11
  88.2 2.3 %copy.12 = f32[2048,128]{1,0:T(8,128)} copy(f32[2048,128]{1,0:T(8,128)} %get-tuple-element.14) | data formatting | bytes 2097152
Async XLA Ops:
  86.2 0.7 copy-start.1
  86.9 0.7 copy-start

commit v2 on v1

--- a/solution.py
+++ b/solution.py
@@ -16,6 +16,8 @@
 LOG2E = math.log2(math.e)
 UNIT = EPSILON / LOG2E
 MESH = pl.DeviceIdType.MESH
+WIDTH, STEP, SUB = 512, 256, 64
+DEPTH = 2048
 
 
 def augment(coords_ref, wide_ref, rows_ref, columns_ref, norm_first):
@@ -60,33 +62,33 @@
 
 def column_pass(tile_ref, bias_ref, lse_ref, make=None):
     rows, columns = tile_ref.shape
-    width = math.gcd(columns, 256)
-    step = math.gcd(rows, 256)
-    sub = math.gcd(step, 128)
+    width = math.gcd(columns, WIDTH)
+    step = math.gcd(rows, STEP)
+    sub = math.gcd(step, SUB)
     halves = width // LANES
 
     def over_columns(c, unused):
         start = pl.multiple_of(c * width, width)
-
-        def over_rows(r, carry):
-            row = pl.multiple_of(r * step, step)
-            if make is not None:
-                tile_ref[pl.ds(row, step), pl.ds(start, width)] = make(
-                    pl.ds(row, step), pl.ds(start, width)
-                )
-            carry = list(carry)
+        lanes = [pl.ds(pl.multiple_of(start + h * LANES, LANES), LANES) for h in range(halves)]
+
+        def fill(r):
+            at = pl.ds(r * step, step)
+            tile_ref[at, pl.ds(start, width)] = make(at, pl.ds(start, width))
+
+        empty = (jnp.full((8, LANES), -jnp.inf, jnp.float32), jnp.zeros((8, LANES), jnp.float32))
+        stats = [empty] * halves
+        if make is not None:
+            fill(0)
+        for r in range(rows // step):
+            if make is not None and r + 1 < rows // step:
+                fill(r + 1)
             for q in range(step // sub):
-                at = pl.ds(pl.multiple_of(row + q * sub, sub), sub)
+                at = pl.ds(r * step + q * sub, sub)
                 for h in range(halves):
-                    lanes = pl.ds(pl.multiple_of(start + h * LANES, LANES), LANES)
-                    block = tile_ref[at, lanes]
+                    block = tile_ref[at, lanes[h]]
                     if bias_ref is not None:
                         block = block + bias_ref[at, :]
-                    carry[h] = join(*carry[h], block)
-            return tuple(carry)
-
-        empty = (jnp.full((8, LANES), -jnp.inf, jnp.float32), jnp.zeros((8, LANES), jnp.float32))
-        stats = lax.fori_loop(0, rows // step, over_rows, (empty,) * halves)
+                    stats[h] = join(*stats[h], block)
         for h in range(halves):
             top, total = closed(*stats[h])
             lse_ref[pl.ds(c * halves + h, 1), :] = top + jnp.log2(total)
@@ -95,10 +97,38 @@
     lax.fori_loop(0, columns // width, over_columns, 0)
 
 
+def carry_tile(tile_ref, bias_ref, scores_ref, weights, start, width):
+    rows = tile_ref.shape[0]
+    halves = width // LANES
+    sub = math.gcd(rows, SUB)
+    step = math.gcd(rows, DEPTH)
+    lanes = [pl.ds(pl.multiple_of(start + h * LANES, LANES), LANES) for h in range(halves)]
+    peaks = [jnp.full((8, LANES), -jnp.inf, jnp.float32)] * halves
+    for r in range(rows // sub):
+        at = pl.ds(r * sub, sub)
+        for h in range(halves):
+            block = tile_ref[at, lanes[h]] + bias_ref[at, :]
+            peaks[h] = jnp.maximum(peaks[h], jnp.max(block.reshape(-1, 8, LANES), axis=0))
+    peaks = [jnp.max(peak, axis=0, keepdims=True) for peak in peaks]
+    totals = [jnp.zeros((8, LANES), jnp.float32)] * halves
+    for r in range(rows // sub):
+        at = pl.ds(r * sub, sub)
+        for h in range(halves):
+            w = jnp.exp2(tile_ref[at, lanes[h]] + bias_ref[at, :] - peaks[h])
+            totals[h] = totals[h] + jnp.sum(w.reshape(-1, 8, LANES), axis=0)
+            weights[at, h * LANES : (h + 1) * LANES] = w.astype(jnp.bfloat16)
+    carried = None
+    for r in range(rows // step):
+        at = slice(r * step, (r + 1) * step)
+        part = jnp.dot(scores_ref[:, at], weights[at, 0:width], preferred_element_type=jnp.float32)
+        carried = part if carried is None else carried + part
+    return peaks, [jnp.sum(total, axis=0, keepdims=True) for total in totals], carried
+
+
 def kernel(
     n_src, n_tgt, xs_ref, yt_ref, growth_ref, scores_ref, f_ref, g_ref, out_ref,
-    tile, tile_t, wide, x_rows, x_cols, y_rows, y_cols, scores_t, bias, weights, carried, partial,
-    lse, row_buf, col_buf, stat, received, row_send, row_recv, col_send, col_recv,
+    tile, tile_t, wide, x_rows, x_cols, y_rows, y_cols, scores_t, bias, weights, partial,
+    row_buf, col_buf, stat, received, row_send, row_recv, col_send, col_recv,
     stat_send, stat_recv, part_send, part_recv, out_send, out_recv,
 ):
     src, tgt = lax.axis_index("src"), lax.axis_index("tgt")
@@ -175,52 +205,17 @@
     f_ref[...] = UNIT * potential
 
     piece = columns // n_src
-    width = math.gcd(piece, 256)
-    depth = math.gcd(rows, 256)
+    width = math.gcd(piece, WIDTH)
     halves = width // LANES
-    sub = math.gcd(depth, 128)
     parts = []
     for k in range(1, n_src + 1):
         owner = lax.rem(src + k, n_src)
 
         def over_tiles(c, unused, owner=owner):
             start = pl.multiple_of(owner * piece + c * width, width)
-
-            def tops(r, peaks):
-                at = pl.ds(pl.multiple_of(r * depth, depth), depth)
-                peaks = list(peaks)
-                for h in range(halves):
-                    lanes = pl.ds(pl.multiple_of(start + h * LANES, LANES), LANES)
-                    block = tile[at, lanes] + bias[at, :]
-                    peaks[h] = jnp.maximum(peaks[h], jnp.max(block.reshape(-1, 8, LANES), axis=0))
-                return tuple(peaks)
-
-            peaks = lax.fori_loop(
-                0, rows // depth, tops,
-                (jnp.full((8, LANES), -jnp.inf, jnp.float32),) * halves,
-            )
-            peaks = [jnp.max(peak, axis=0, keepdims=True) for peak in peaks]
-
-            def plan(r, totals):
-                row = pl.multiple_of(r * depth, depth)
-                totals = list(totals)
-                for q in range(depth // sub):
-                    at = pl.ds(pl.multiple_of(row + q * sub, sub), sub)
-                    for h in range(halves):
-                        lanes = pl.ds(pl.multiple_of(start + h * LANES, LANES), LANES)
-                        w = jnp.exp2(tile[at, lanes] + bias[at, :] - peaks[h])
-                        totals[h] = totals[h] + jnp.sum(w.reshape(-1, 8, LANES), axis=0)
-                        weights[at, h * LANES : (h + 1) * LANES] = w.astype(jnp.bfloat16)
-                return tuple(totals)
-
-            totals = lax.fori_loop(
-                0, rows // depth, plan, (jnp.zeros((8, LANES), jnp.float32),) * halves
-            )
-            carried[...] = jnp.dot(scores_t[...], weights[...], preferred_element_type=jnp.float32)
+            peaks, totals, carried = carry_tile(tile, bias, scores_t, weights, start, width)
             for h in range(halves):
-                stat[src, 0, pl.ds(start // LANES + h, 1), :] = jnp.sum(
-                    totals[h], axis=0, keepdims=True
-                )
+                stat[src, 0, pl.ds(start // LANES + h, 1), :] = totals[h]
                 stat[src, 1, pl.ds(start // LANES + h, 1), :] = peaks[h]
                 at = pl.ds(pl.multiple_of(start + h * LANES, LANES), LANES)
                 partial[at, :] = carried[:, h * LANES : (h + 1) * LANES].T
@@ -302,10 +297,8 @@
                 pltpu.VMEM((LANES, columns), bf16),
                 pltpu.VMEM((programs, rows), bf16),
                 pltpu.VMEM((max(rows, columns), LANES), f32),
-                pltpu.VMEM((rows, math.gcd(piece, 256)), bf16),
-                pltpu.VMEM((programs, math.gcd(piece, 256)), f32),
+                pltpu.VMEM((rows, math.gcd(piece, WIDTH)), bf16),
                 pltpu.VMEM((columns, programs), f32),
-                pltpu.VMEM((8, LANES), f32),
                 pltpu.VMEM((ITERS, n_tgt) + dense_r, f32),
                 pltpu.VMEM((ITERS, n_src) + dense_c, f32),
                 pltpu.VMEM((n_src, 2) + dense_c, f32),

time: 90.7 us -> 68.5 us (0.76)
  Pallas kernels: 85.6 us -> 63.4 us
    pallas_call x1, Pallas kernels: 85.6 us -> 63.4 us  [shards(): pl.pallas_call(functools.partial(kernel, n_src, n_tgt), out_shape=(jax.Sh...]
where the time goes in v2:
time: 68.5 us; the launch traced here: 68.3 us
  Pallas kernels  63.4 us (93%)
  local copies, waits for them, and re-layouts  4.25 us (6%)
    pallas_call x1, Pallas kernels, shards(): pl.pallas_call(functools.partial(kernel, n_src, n_tgt), out_shape=(jax.Sh...  63.4 us
    unnamed x7, local copies, waits for them, and re-layouts  4.25 us

profile of v2, /device:TPU:0, one launch (start us, length us, event | category | flops | bytes accessed | tf_op | source)
XLA Modules:
  0.0 68.3 jit_solution(8162551155680361208)
XLA Ops:
  0.6 63.4 %coupling.1 = (f32[16,128]{1,0:T(8,128)}, f32[16,128]{1,0:T(8,128)}, f32[2048,128]{1,0:T(8,128)}) custom-call(bf16[30,2048]{1,0:T(8,128)(2,1)} %xs_ref.1, bf16[30,2048]{1,0:T(8,128)(2,1)} %yt_ref.1, f32[16,128]{1,0:T(8,128)} %bitcast.3, bf16[2048,128]{1,0:T(8,128)(2,1)} %scores_ref.1), custom_call_target="tpu_custom_call" | custom-call | tf_op jit(solution)/shard_map/coupling/pallas_call | solution.py:281
  64.0 0.0 copy-start.1
  64.0 0.7 %copy-done.1 = f32[16,128]{1,0:T(8,128)S(1)} copy-done((f32[16,128]{1,0:T(8,128)S(1)}, f32[16,128]{1,0:T(8,128)}, u32[]{:S(2)}) %copy-start.1) | copy-done | bytes 8216
  64.7 0.0 copy-start
  64.7 0.6 copy.10
  65.3 0.1 copy-done
  65.4 0.6 copy.11
  66.0 2.3 %copy.12 = f32[2048,128]{1,0:T(8,128)} copy(f32[2048,128]{1,0:T(8,128)} %get-tuple-element.14) | data formatting | bytes 2097152
Async XLA Ops:
  64.0 0.7 %copy-start.1 = (f32[16,128]{1,0:T(8,128)S(1)}, f32[16,128]{1,0:T(8,128)}, u32[]{:S(2)}) copy-start(f32[16,128]{1,0:T(8,128)} %get-tuple-element.6) | copy-start | bytes 24580
  64.7 0.7 %copy-start = (f32[16,128]{1,0:T(8,128)S(1)}, f32[16,128]{1,0:T(8,128)}, u32[]{:S(2)}) copy-start(f32[16,128]{1,0:T(8,128)} %get-tuple-element.7) | copy-start | bytes 24580
